TPU v7x, 128 devices: a whole 4x4x4 slice. The times are simulated.
128 devices in a mesh: ctx: 64 (over z, x, y), wsh: 2 (over core).
Axes of the slice: x: 4, y: 4, z: 4, core: 2. Of those that a mesh axis runs over, the one named last changes fastest.
Arguments:
- block_input: bfloat16 [2, 8192, 640], P('wsh', 'ctx'), may hold values from -6 to 6
- cotangent: float32 [2, 8192, 640], P('wsh', 'ctx'), may hold values from -6 to 6
- pair_blocks: int32 [64, 2], replicated, may hold values from 0 to 127, as said below
- w_query: bfloat16 [640, 1024], P(None, 'wsh'), may hold values from -0.25 to 0.25
- w_key: bfloat16 [640, 256], P(None, 'wsh'), may hold values from -0.25 to 0.25
- w_value: bfloat16 [640, 256], P(None, 'wsh'), may hold values from -0.25 to 0.25
- w_out: bfloat16 [1024, 640], P('wsh'), may hold values from -0.1875 to 0.1875
- w_gate: bfloat16 [640, 2048], P(None, 'wsh'), may hold values from -0.25 to 0.25
- w_up: bfloat16 [640, 2048], P(None, 'wsh'), may hold values from -0.25 to 0.25
- w_down: bfloat16 [2048, 640], P('wsh'), may hold values from -0.125 to 0.125
- attn_pre_gain: bfloat16 [640], P('wsh'), may hold values from -0.3984375 to 0.59765625
- query_gain: bfloat16 [256], P('wsh'), may hold values from -0.3984375 to 0.59765625
- key_gain: bfloat16 [256], P('wsh'), may hold values from -0.3984375 to 0.59765625
- attn_post_gain: bfloat16 [640], P('wsh'), may hold values from -0.3984375 to 0.59765625
- ffw_pre_gain: bfloat16 [640], P('wsh'), may hold values from -0.3984375 to 0.59765625
- ffw_post_gain: bfloat16 [640], P('wsh'), may hold values from -0.3984375 to 0.59765625
Outputs:
- block_output: float32 [2, 8192, 640], P('wsh', 'ctx')
- input_grad: float32 [2, 8192, 640], P('wsh', 'ctx')
- w_query_grad: float32 [640, 1024], P(None, 'wsh')
- w_key_grad: float32 [640, 256], P(None, 'wsh')
- w_value_grad: float32 [640, 256], P(None, 'wsh')
- w_out_grad: float32 [1024, 640], P('wsh')
- w_gate_grad: float32 [640, 2048], P(None, 'wsh')
- w_up_grad: float32 [640, 2048], P(None, 'wsh')
- w_down_grad: float32 [2048, 640], P('wsh')
- attn_pre_gain_grad: float32 [640], P('wsh')
- query_gain_grad: float32 [256], P('wsh')
- key_gain_grad: float32 [256], P('wsh')
- attn_post_gain_grad: float32 [640], P('wsh')
- ffw_pre_gain_grad: float32 [640], P('wsh')
- ffw_post_gain_grad: float32 [640], P('wsh')
Inputs may be any that keep to these rules, and one draw needn't show every extreme that they name: `pair_blocks`: row r holds a block b and its mirror 2 * 64 - 1 - b, in the order in which index r of ctx stores them; over all rows every one of the 128 blocks appears exactly once.
All inputs are finite; a program needn't handle non-finite values.
Results may differ from a plain program's by a relative error of at most 0.018.
Values may be sent and summed in bfloat16 or wider, within the bound.
No kernel may reach another device: no remote copies, remote signals or barrier semaphores. Data moves between devices by JAX's collectives and lax.ppermute only.
A program may use at most 192 MiB of HBM per device.

v0:
```python
import jax
import jax.numpy as jnp
from jax import lax
from jax.sharding import Mesh
from jax.sharding import PartitionSpec as P

HEADS = 4
HDIM = 256
CTX = ("z", "x", "y")
epsilon = 1e-06
theta_base = 1000000.0
bf16 = jnp.bfloat16
f32 = jnp.float32


def rms_forward(values, gain_w):
    factor = lax.rsqrt(jnp.mean(values * values, axis=-1, keepdims=True) + epsilon)
    return (values * factor * (1.0 + gain_w), factor)


def rms_backward(values, factor, gain_w, grad_out):
    weighted = grad_out * (1.0 + gain_w)
    inner = jnp.mean(weighted * values, axis=-1, keepdims=True)
    grad_in = factor * (weighted - values * factor * factor * inner)
    grad_gain = jnp.sum((grad_out * values * factor).reshape(-1, values.shape[-1]), axis=0)
    return (grad_in, grad_gain)


def rotary_tables(positions, width):
    half_width = width // 2
    frequency = theta_base ** (-jnp.arange(half_width, dtype=f32) * 2.0 / width)
    angles = positions.astype(f32)[:, None] * frequency[None, :]
    return (jnp.cos(angles), jnp.sin(angles))


def rotate(values, cos_tab, sin_tab):
    half = values.shape[-1] // 2
    a, b = (values[..., :half], values[..., half:])
    return jnp.concatenate([a * cos_tab - b * sin_tab, b * cos_tab + a * sin_tab], axis=-1)


def rotate_back(grads, cos_tab, sin_tab):
    half = grads.shape[-1] // 2
    a, b = (grads[..., :half], grads[..., half:])
    return jnp.concatenate([a * cos_tab + b * sin_tab, b * cos_tab - a * sin_tab], axis=-1)


def block_positions(block_ids, half_rows):
    offsets = jnp.arange(half_rows, dtype=jnp.int32)
    return (block_ids[:, None] * half_rows + offsets[None, :]).reshape(-1)


def dot_f32(left, right):
    return jnp.dot(left, right, preferred_element_type=f32)


def dot_nt(left, right):
    return lax.dot_general(left, right, (((1,), (1,)), ((), ())), preferred_element_type=f32)


def dot_tn(left, right):
    return lax.dot_general(left, right, (((0,), (0,)), ((), ())), preferred_element_type=f32)


def swap(values):
    return lax.ppermute(values, "wsh", [(0, 1), (1, 0)])


def attention_forward(query, keys, vals, query_pos, key_pos):
    scores = dot_nt(query, keys) * HDIM ** (-0.5)
    scores = jnp.where(key_pos[None, :] <= query_pos[:, None], scores, -1e30)
    top = jnp.max(scores, axis=-1, keepdims=True)
    shifted = jnp.exp(scores - top)
    totals = jnp.sum(shifted, axis=-1, keepdims=True)
    probs = (shifted / totals).astype(bf16)
    return (dot_f32(probs, vals).astype(bf16), top + jnp.log(totals))


def attention_backward(query, keys, vals, query_pos, key_pos, grads, log_total, delta):
    scores = dot_nt(query, keys) * HDIM ** (-0.5)
    scores = jnp.where(key_pos[None, :] <= query_pos[:, None], scores, -1e30)
    probs = jnp.exp(scores - log_total)
    grad_probs = dot_nt(grads, vals)
    grad_scores = (probs * (grad_probs - delta)).astype(bf16)
    grad_query = dot_f32(grad_scores, keys) * HDIM ** (-0.5)
    grad_key = dot_tn(grad_scores, query) * HDIM ** (-0.5)
    grad_value = dot_tn(probs.astype(bf16), grads)
    return (grad_query, jnp.concatenate([grad_key.astype(bf16), grad_value.astype(bf16)], axis=1))


def gather_ctx(block):
    return lax.all_gather(block, CTX, axis=0, tiled=True)


def scatter_sum(parts):
    got = lax.all_to_all(parts.reshape(64, 128, -1), CTX, split_axis=0, concat_axis=0, tiled=True)
    return jnp.sum(got.astype(f32), axis=0)


def small_sum(values):
    rows = values.shape[0] // 64
    got = lax.all_to_all(values.reshape(64, rows, -1), CTX, split_axis=0, concat_axis=0, tiled=True)
    mine = jnp.sum(got.astype(f32), axis=0).astype(values.dtype)
    wide = jnp.broadcast_to(mine[None], (64,) + mine.shape)
    out = lax.all_to_all(wide, CTX, split_axis=0, concat_axis=0, tiled=True)
    return out.reshape(values.shape)


def per_device(
    block_input,
    cotangent,
    pair_blocks,
    w_query,
    w_key,
    w_value,
    w_out,
    w_gate,
    w_up,
    w_down,
    attn_pre_gain,
    query_gain,
    key_gain,
    attn_post_gain,
    ffw_pre_gain,
    ffw_post_gain,
):
    rows = block_input.shape[1]
    rank = lax.axis_index(CTX)
    first = lax.axis_index("wsh") == 0

    def ordered(own, other, axis):
        return jnp.where(
            first,
            jnp.concatenate([own, other], axis=axis),
            jnp.concatenate([other, own], axis=axis),
        )

    resid_in = block_input[0].astype(f32)
    grad_top = cotangent[0]
    query_pos = block_positions(lax.dynamic_slice_in_dim(pair_blocks, rank, 1, 0)[0], rows // 2)
    key_pos = block_positions(pair_blocks.reshape(-1), rows // 2)
    cos_tab, sin_tab = rotary_tables(query_pos, HDIM)
    gains_own = jnp.concatenate(
        [attn_pre_gain, attn_post_gain, ffw_pre_gain, ffw_post_gain, query_gain, key_gain]
    )[None]
    gains_other = swap(gains_own)
    kv_own = jnp.concatenate([w_key, w_value], axis=1)
    kv_other = swap(kv_own)

    def gain(start, width):
        return ordered(
            gains_own[0, start : start + width], gains_other[0, start : start + width], 0
        ).astype(f32)[None]

    gain_one, gain_two, gain_three, gain_four = (gain(320 * i, 320) for i in range(4))
    gain_query, gain_key = (gain(1280, 128), gain(1408, 128))
    key_w = ordered(kv_own[:, :128], kv_other[:, :128], 1)
    value_w = ordered(kv_own[:, 128:], kv_other[:, 128:], 1)
    normed_one, factor_one = rms_forward(resid_in, gain_one)
    attn_in = normed_one.astype(bf16)
    key_raw = dot_f32(attn_in, key_w)
    value_bf = dot_f32(attn_in, value_w).astype(bf16)
    key_normed, key_factor = rms_forward(key_raw, gain_key)
    key_rot = rotate(key_normed, cos_tab, sin_tab).astype(bf16)
    kv_all = gather_ctx(jnp.concatenate([key_rot, value_bf], axis=1))
    key_all, value_all = (kv_all[:, :HDIM], kv_all[:, HDIM:])
    query_w = (w_query, swap(w_query))
    out_w = (w_out, swap(w_out))
    gate_w = (w_gate, swap(w_gate))
    up_w = (w_up, swap(w_up))
    down_w = (w_down, swap(w_down))

    def heads_first(pair):
        return jnp.concatenate(
            [half[:, HDIM * h : HDIM * (h + 1)] for half in pair for h in range(2)], axis=0
        )

    def heads_last(stacked):
        return tuple(
            (
                jnp.concatenate(
                    [stacked[rows * h : rows * (h + 1)] for h in (2 * p, 2 * p + 1)], axis=1
                )
                for p in range(2)
            )
        )

    cos4, sin4 = (jnp.tile(cos_tab, (HEADS, 1)), jnp.tile(sin_tab, (HEADS, 1)))
    query_raw = heads_first(tuple((dot_f32(attn_in, half) for half in query_w)))
    query_normed, query_factor = rms_forward(query_raw, gain_query)
    query_rot = rotate(query_normed, cos4, sin4).astype(bf16)
    pos4 = jnp.tile(query_pos, HEADS)
    attn_heads, log_total = attention_forward(query_rot, key_all, value_all, pos4, key_pos)
    attn_out = heads_last(attn_heads)
    attn_proj = dot_f32(attn_out[0], out_w[0]) + dot_f32(attn_out[1], out_w[1])
    normed_two, factor_two = rms_forward(attn_proj, gain_two)
    mid = resid_in + normed_two
    normed_three, factor_three = rms_forward(mid, gain_three)
    ffw_in = normed_three.astype(bf16)
    gate = [dot_f32(ffw_in, half) for half in gate_w]
    up_val = [dot_f32(ffw_in, half) for half in up_w]
    acts = [jax.vjp(lambda inner: jax.nn.gelu(inner, approximate=True), g) for g in gate]
    hidden = [(act[0] * up).astype(bf16) for act, up in zip(acts, up_val)]
    ffw_proj = dot_f32(hidden[0], down_w[0]) + dot_f32(hidden[1], down_w[1])
    normed_four, factor_four = rms_forward(ffw_proj, gain_four)
    block_output = mid + normed_four
    grad_ffw, grad_gain_four = rms_backward(ffw_proj, factor_four, gain_four, grad_top)
    grad_ffw_bf = grad_ffw.astype(bf16)
    grad_hidden = [dot_nt(grad_ffw_bf, half) for half in down_w]
    grad_gate = [act[1](gh * up)[0].astype(bf16) for act, gh, up in zip(acts, grad_hidden, up_val)]
    grad_up = [(gh * act[0]).astype(bf16) for act, gh in zip(acts, grad_hidden)]
    grad_ffw_in = (
        dot_nt(grad_gate[0], gate_w[0])
        + dot_nt(grad_gate[1], gate_w[1])
        + dot_nt(grad_up[0], up_w[0])
        + dot_nt(grad_up[1], up_w[1])
    )
    grad_mid_part, grad_gain_three = rms_backward(mid, factor_three, gain_three, grad_ffw_in)
    grad_mid = grad_top + grad_mid_part
    grad_proj, grad_gain_two = rms_backward(attn_proj, factor_two, gain_two, grad_mid)
    grad_proj_bf = grad_proj.astype(bf16)
    grad_attn = tuple((dot_nt(grad_proj_bf, half).astype(bf16) for half in out_w))
    grad_heads = heads_first(grad_attn)

    def both(own, other):
        return jnp.concatenate([own, swap(other)], axis=0)

    ffw_in2 = both(ffw_in, ffw_in)
    grad_w_down = dot_tn(both(hidden[0], hidden[1]), both(grad_ffw_bf, grad_ffw_bf))
    grad_w_gate = dot_tn(ffw_in2, both(grad_gate[0], grad_gate[1]))
    grad_w_up = dot_tn(ffw_in2, both(grad_up[0], grad_up[1]))
    grad_w_out = dot_tn(both(attn_out[0], attn_out[1]), both(grad_proj_bf, grad_proj_bf))
    attn_in2 = both(attn_in, attn_in)
    delta = jnp.sum(grad_heads.astype(f32) * attn_heads.astype(f32), axis=-1, keepdims=True)
    grad_query, kv_terms = attention_backward(
        query_rot, key_all, value_all, pos4, key_pos, grad_heads, log_total, delta
    )
    grad_query_raw, grad_gain_query = rms_backward(
        query_raw, query_factor, gain_query, rotate_back(grad_query, cos4, sin4)
    )
    grad_query_bf = heads_last(grad_query_raw.astype(bf16))
    grad_w_query = dot_tn(attn_in2, both(grad_query_bf[0], grad_query_bf[1]))
    big = tuple(
        (g.astype(bf16) for g in (grad_w_query, grad_w_out, grad_w_gate, grad_w_up, grad_w_down))
    )
    sum_query, sum_out, sum_gate, sum_up, sum_down = (g.astype(f32) for g in lax.psum(big, CTX))
    kv_mine = scatter_sum(kv_terms)
    grad_key_raw, grad_gain_key = rms_backward(
        key_raw, key_factor, gain_key, rotate_back(kv_mine[:, :HDIM], cos_tab, sin_tab)
    )
    grad_key_bf = grad_key_raw.astype(bf16)
    grad_value_bf = kv_mine[:, HDIM:].astype(bf16)

    def mine_other(full):
        a, b = (full[:, :128], full[:, 128:])
        return (jnp.where(first, a, b), jnp.where(first, b, a))

    key_m, key_o = mine_other(grad_key_bf)
    val_m, val_o = mine_other(grad_value_bf)
    grad_kv2 = both(
        jnp.concatenate([key_m, val_m], axis=1), jnp.concatenate([key_o, val_o], axis=1)
    )
    grad_w_kv = dot_tn(grad_kv2, attn_in2)
    grad_attn_in = (
        dot_nt(grad_query_bf[0], query_w[0])
        + dot_nt(grad_query_bf[1], query_w[1])
        + dot_nt(grad_key_bf, key_w)
        + dot_nt(grad_value_bf, value_w)
    )
    grad_in_part, grad_gain_one = rms_backward(resid_in, factor_one, gain_one, grad_attn_in)
    input_grad = grad_mid + grad_in_part
    gain_grads = (
        grad_gain_one,
        grad_gain_two,
        grad_gain_three,
        grad_gain_four,
        grad_gain_query,
        grad_gain_key,
    )
    g_own = jnp.concatenate(
        [jnp.where(first, g[: g.size // 2], g[g.size // 2 :]) for g in gain_grads]
    )
    g_other = jnp.concatenate(
        [jnp.where(first, g[g.size // 2 :], g[: g.size // 2]) for g in gain_grads]
    )
    g_sum = g_own + swap(g_other[None])[0]
    g_block = jnp.concatenate([g_sum, jnp.zeros((1024,), f32)]).reshape(64, 40).astype(bf16)
    late = jnp.concatenate([grad_w_kv.astype(bf16).reshape(64, 2560), g_block], axis=1)
    late = small_sum(late).astype(f32)
    sum_kv = late[:, :2560].reshape(256, 640)
    sum_gains = late[:, 2560:].reshape(-1)
    return (
        block_output[None],
        input_grad[None],
        sum_query,
        sum_kv[:128].T,
        sum_kv[128:].T,
        sum_out,
        sum_gate,
        sum_up,
        sum_down,
        sum_gains[:320],
        sum_gains[1280:1408],
        sum_gains[1408:1536],
        sum_gains[320:640],
        sum_gains[640:960],
        sum_gains[960:1280],
    )


def solution(mesh):
    grid = Mesh(mesh.devices.reshape(4, 4, 4, 2), ("z", "x", "y", "wsh"))
    tokens = P("wsh", CTX, None)
    cols, rows, vec = (P(None, "wsh"), P("wsh", None), P("wsh"))
    return jax.shard_map(
        per_device,
        mesh=grid,
        in_specs=(tokens, tokens, P(), cols, cols, cols, rows, cols, cols, rows) + (vec,) * 6,
        out_specs=(tokens, tokens, cols, cols, cols, rows, cols, cols, rows) + (vec,) * 6,
        check_vma=False,
    )
```

profile of v0, /device:TPU:0, one launch (start us, length us, event | category | flops | bytes accessed | tf_op | source)
XLA Modules:
  0.0 476.8 jit_solution(2237025595340672218)
XLA Ops:
  7.2 4.3 concatenate.211
  26.4 75.5 %all-gather.2.cloned.1.call-done = bf16[8192,512]{1,0:T(8,128)(2,1)} async-done(((bf16[128,512]{1,0:T(8,128)(2,1)}), bf16[8192,512]{1,0:T(8,128)(2,1)}) %all-gather.2.cloned.1.call-update) | async-done | bytes 8388624 | tf_op jit(solution)/shard_map/all_gather | solution.py:92
  101.9 10.8 %fusion.133 = (f32[512]{0:T(512)S(1)}, f32[512,8192]{1,0:T(8,128)}) fusion(bf16[8192,512]{1,0:T(8,128)(2,1)} %all-gather.2.cloned.1.call-done, bf16[512,128]{1,0:T(8,128)(2,1)} %get-tuple-element.99, bf16[512,128]{1,0:T(8,128)(2,1)S(1)} %get-tuple-element.98, s32[512]{0:T(512)S(1)} %broadcast_bitcast_fusion, s32[8192]{0:T(1024)S(1)} %add.247), kind=kOutput, calls=%fused_computation.278 | convolution fusion | flops 2164784640 | bytes 21270528 | tf_op jit(solution)/shard_map/dot_general | solution.py:58
  112.8 8.1 %fusion = f32[512]{0:T(512)S(1)} fusion(f32[512,8192]{1,0:T(8,128)} %get-tuple-element.159, f32[512]{0:T(512)S(1)} %get-tuple-element.158), kind=kLoop, calls=%fused_computation.6 | loop fusion | flops 8388096 | bytes 16781312 | tf_op jit(solution)/shard_map/reduce_sum | solution.py:74
  120.9 10.0 %fusion.14 = bf16[512,256]{0,1:T(8,128)(2,1)S(1)} fusion(bf16[8192,512]{1,0:T(8,128)(2,1)} %all-gather.2.cloned.1.call-done, f32[512,8192]{1,0:T(8,128)} %get-tuple-element.159, f32[512]{0:T(512)S(1)} %fusion, f32[512]{0:T(512)S(1)} %get-tuple-element.158), kind=kOutput, calls=%fused_computation.27 | convolution fusion | flops 2160197632 | bytes 21237760 | tf_op jit(solution)/shard_map/dot_general | solution.py:54
  134.4 1.7 fusion.136
  137.0 1.8 fusion.138
  139.3 1.9 multiply_reduce_fusion.9
  143.6 2.0 fusion.139
  145.7 2.2 multiply_convert_fusion.2
  147.9 2.1 convolution_add_fusion.5
  156.1 5.2 %convolution_convert_fusion = bf16[8192,256]{0,1:T(8,128)(2,1)} fusion(f32[512,8192]{1,0:T(8,128)S(1)} %bitcast.112, f32[512]{0:T(512)S(1)} %log_add_fusion, bf16[128,256]{0,1:T(8,128)(2,1)S(1)} %get-tuple-element.131, bf16[128,256]{0,1:T(8,128)(2,1)S(1)} %get-tuple-element.130, bf16[128,256]{0,1:T(8,128)(2,1)} %copy-done.20, bf16[128,256]{0,1:T(8,128)(2,1)} %copy-done.19), kind=kOutput, calls=%fused_computation.8 | convolution fusion | flops 2159017984 | bytes 21235712 | tf_op jit(solution)/shard_map/dot_general | solution.py:62
  161.3 10.0 %multiply_convert_fusion = bf16[512,8192]{1,0:T(8,128)(2,1)S(1)} fusion(f32[512,8192]{1,0:T(8,128)} %get-tuple-element.159, f32[512]{0:T(512)S(1)} %multiply_reduce_fusion.2, f32[512]{0:T(512)S(1)} %log_add_fusion, bf16[8192,512]{1,0:T(8,128)(2,1)} %all-gather.2.cloned.1.call-done, bf16[128,256]{0,1:T(8,128)(2,1)S(1)} %get-tuple-element.131, ...), kind=kOutput, calls=%fused_computation.1 | convolution fusion | flops 2165309440 | bytes 29626368 | tf_op jit(solution)/shard_map/dot_general | solution.py:58
  171.3 2.4 fusion.2
  173.7 1.8 copy-done.1
  176.6 4.4 copy_bitcast_fusion
  181.0 9.0 %all-to-all-start = ((bf16[64,128,512]{1,2,0:T(8,128)(2,1)}), bf16[64,128,512]{1,2,0:T(8,128)(2,1)}, u32[]{:S(2)}, u32[]{:S(2)}) async-start(bf16[64,128,512]{1,2,0:T(8,128)(2,1)} %copy_bitcast_fusion), calls=%async_computation | async-start | bytes 16777216 | tf_op jit(solution)/shard_map/all_to_all | solution.py:96
  190.2 6.9 %fusion.11 = f32[512,256]{1,0:T(8,128)S(1)} fusion(bf16[512,8192]{1,0:T(8,128)(2,1)} %copy-done.1, bf16[8192,512]{1,0:T(8,128)(2,1)} %all-gather.2.cloned.1.call-done), kind=kOutput, calls=%fused_computation.26 | convolution fusion | flops 2147614720 | bytes 13107200 | tf_op jit(solution)/shard_map/dot_general | solution.py:54
  203.0 1.6 convolution_convert_fusion.3
  206.2 1.7 convolution_convert_fusion.1
  211.0 97.9 %all-to-all-done = bf16[64,128,512]{1,2,0:T(8,128)(2,1)} async-done(((bf16[64,128,512]{1,2,0:T(8,128)(2,1)}), bf16[64,128,512]{1,2,0:T(8,128)(2,1)}, u32[]{:S(2)}, u32[]{:S(2)}) %all-to-all-start) | async-done | bytes 8388640 | tf_op jit(solution)/shard_map/all_to_all | solution.py:96
  308.9 4.8 convert_reduce_fusion
  319.9 8.7 %all-to-all-start.1 = ((bf16[64,2,1300]{2,1,0:T(2,128)(2,1)}), bf16[64,2,1300]{2,1,0:T(2,128)(2,1)S(1)}, u32[]{:S(2)}, u32[]{:S(2)}) async-start(bf16[64,2,1300]{2,1,0:T(2,128)(2,1)} %reshape.477), calls=%async_computation.1 | async-start | bytes 720896 | tf_op jit(solution)/shard_map/all_to_all | solution.py:102
  328.7 100.5 %all-reduce.4.cloned.1.call-done = (bf16[640,512]{1,0:T(8,128)(2,1)}, bf16[512,640]{1,0:T(8,128)(2,1)}, bf16[640,1024]{1,0:T(8,128)(2,1)}, bf16[640,1024]{1,0:T(8,128)(2,1)}, bf16[1024,640]{1,0:T(8,128)(2,1)}) async-done(((bf16[640,512]{1,0:T(8,128)(2,1)}, bf16[512,640]{1,0:T(8,128)(2,1)}, bf16[640,1024]{1,0:T(8,128)(2,1)}, bf16[640,1024]{1,0:T(8,128)(2,1)}, bf16[1024,640]{1,0:T(8,128)(2,1)}), ...) | async-done | bytes 5242896 | tf_op jit(solution)/shard_map/psum | solution.py:246
  429.2 2.5 convert_element_type.209
  431.7 2.2 convert_element_type.215
  433.9 1.8 convert_element_type.217
  435.7 1.8 convert_element_type.219
  437.5 1.7 convert_element_type.221
  440.7 2.8 reduce.22
  444.6 7.7 %all-to-all-start.2 = ((bf16[64,2,1300]{2,1,0:T(2,128)(2,1)}), bf16[64,2,1300]{2,1,0:T(2,128)(2,1)S(1)}, u32[]{:S(2)}, u32[]{:S(2)}) async-start(bf16[64,2,1300]{2,1,0:T(2,128)(2,1)} %reshape.479), calls=%async_computation.2 | async-start | bytes 720896 | tf_op jit(solution)/shard_map/all_to_all | solution.py:105
  453.2 10.7 %all-to-all-done.2 = bf16[64,2,1300]{2,1,0:T(2,128)(2,1)S(1)} async-done(((bf16[64,2,1300]{2,1,0:T(2,128)(2,1)}), bf16[64,2,1300]{2,1,0:T(2,128)(2,1)S(1)}, u32[]{:S(2)}, u32[]{:S(2)}) %all-to-all-start.2) | async-done | bytes 332832 | tf_op jit(solution)/shard_map/all_to_all | solution.py:105
  (323 shorter events, 54.3 us)
Async XLA Ops:
  7.2 94.7 %all-gather.2.cloned.1.call-start = ((), (), s32[]{:S(2)}) async-start(), calls=%async_computation.3 | async-start | bytes 8519680 | tf_op jit(solution)/shard_map/all_gather | solution.py:92
  11.5 3.9 collective-permute-start
  12.7 4.0 collective-permute-start.2
  20.6 3.4 collective-permute-start.1
  20.7 111.9 %collective-permute-start.3 = (bf16[512,640]{1,0:T(8,128)(2,1)}, bf16[512,640]{1,0:T(8,128)(2,1)}, u32[]{:S(2)}, u32[]{:S(2)}) collective-permute-start(bf16[512,640]{1,0:T(8,128)(2,1)} %param.22), channel_id=1, source_target_pairs={{0,1},{1,0},{2,3},{3,2},{4,5},{5,4},{6,7},{7,6},{8,9},{9,8},{10,11... | collective-permute-start | bytes 1966088 | tf_op jit(solution)/shard_map/ppermute | solution.py:66
  21.2 115.8 %collective-permute-start.4 = (bf16[640,1024]{1,0:T(8,128)(2,1)}, bf16[640,1024]{1,0:T(8,128)(2,1)}, u32[]{:S(2)}, u32[]{:S(2)}) collective-permute-start(bf16[640,1024]{1,0:T(8,128)(2,1)} %param.23), channel_id=1, source_target_pairs={{0,1},{1,0},{2,3},{3,2},{4,5},{5,4},{6,7},{7,6},{8,9},{9,8},{10,11... | collective-permute-start | bytes 3932168 | tf_op jit(solution)/shard_map/ppermute | solution.py:66
  21.4 117.5 %collective-permute-start.5 = (bf16[640,1024]{1,0:T(8,128)(2,1)S(1)}, bf16[640,1024]{1,0:T(8,128)(2,1)S(1)}, u32[]{:S(2)}, u32[]{:S(2)}) collective-permute-start(bf16[640,1024]{1,0:T(8,128)(2,1)S(1)} %copy-done.2), channel_id=1, source_target_pairs={{0,1},{1,0},{2,3},{3,2},{4,5},{5,4},{6,7},{7,6},{8,9},{9,8},{10,11... | collective-permute-start | bytes 3932168 | tf_op jit(solution)/shard_map/ppermute | solution.py:66
  21.8 117.5 %collective-permute-start.6 = (bf16[1024,640]{1,0:T(8,128)(2,1)}, bf16[1024,640]{1,0:T(8,128)(2,1)}, u32[]{:S(2)}, u32[]{:S(2)}) collective-permute-start(bf16[1024,640]{1,0:T(8,128)(2,1)} %param.25), channel_id=1, source_target_pairs={{0,1},{1,0},{2,3},{3,2},{4,5},{5,4},{6,7},{7,6},{8,9},{9,8},{10,11... | collective-permute-start | bytes 3932168 | tf_op jit(solution)/shard_map/ppermute | solution.py:66
  181.0 127.9 %all-to-all-start = ((bf16[64,128,512]{1,2,0:T(8,128)(2,1)}), bf16[64,128,512]{1,2,0:T(8,128)(2,1)}, u32[]{:S(2)}, u32[]{:S(2)}) async-start(bf16[64,128,512]{1,2,0:T(8,128)(2,1)} %copy_bitcast_fusion), calls=%async_computation | async-start | bytes 16777216 | tf_op jit(solution)/shard_map/all_to_all | solution.py:96
  190.0 239.2 %all-reduce.4.cloned.1.call-start = ((), (), s32[]{:S(2)}) async-start(), calls=%async_computation.4 | async-start | bytes 10485760 | tf_op jit(solution)/shard_map/psum | solution.py:246
  190.1 9.1 %collective-permute-start.7 = (bf16[128,640]{1,0:T(8,128)(2,1)S(1)}, bf16[128,640]{1,0:T(8,128)(2,1)S(1)}, u32[]{:S(2)}, u32[]{:S(2)}) collective-permute-start(bf16[128,640]{1,0:T(8,128)(2,1)S(1)} %copy-done.10), channel_id=1, source_target_pairs={{0,1},{1,0},{2,3},{3,2},{4,5},{5,4},{6,7},{7,6},{8,9},{9,8},{10,11... | collective-permute-start | bytes 491528 | tf_op jit(solution)/shard_map/ppermute | solution.py:66
  197.9 1.7 collective-permute-start.8
  198.5 2.9 collective-permute-start.12
  198.6 4.4 collective-permute-start.14
  199.0 2.0 collective-permute-start.11
  199.2 3.8 collective-permute-start.13
  199.6 4.9 %collective-permute-start.15 = (bf16[128,1024]{1,0:T(8,128)(2,1)S(1)}, bf16[128,1024]{1,0:T(8,128)(2,1)S(1)}, u32[]{:S(2)}, u32[]{:S(2)}) collective-permute-start(bf16[128,1024]{1,0:T(8,128)(2,1)S(1)} %copy-done.38), channel_id=1, source_target_pairs={{0,1},{1,0},{2,3},{3,2},{4,5},{5,4},{6,7},{7,6},{8,9},{9,8},{10,11... | collective-permute-start | bytes 786440 | tf_op jit(solution)/shard_map/ppermute | solution.py:66
  201.1 5.1 %collective-permute-start.16 = (bf16[128,1024]{1,0:T(8,128)(2,1)S(1)}, bf16[128,1024]{1,0:T(8,128)(2,1)S(1)}, u32[]{:S(2)}, u32[]{:S(2)}) collective-permute-start(bf16[128,1024]{1,0:T(8,128)(2,1)S(1)} %copy-done.24), channel_id=1, source_target_pairs={{0,1},{1,0},{2,3},{3,2},{4,5},{5,4},{6,7},{7,6},{8,9},{9,8},{10,11... | collective-permute-start | bytes 786440 | tf_op jit(solution)/shard_map/ppermute | solution.py:66
  201.4 4.8 %collective-permute-start.17 = (bf16[128,640]{1,0:T(8,128)(2,1)S(1)}, bf16[128,640]{1,0:T(8,128)(2,1)S(1)}, u32[]{:S(2)}, u32[]{:S(2)}) collective-permute-start(bf16[128,640]{1,0:T(8,128)(2,1)S(1)} %copy-done.54), channel_id=1, source_target_pairs={{0,1},{1,0},{2,3},{3,2},{4,5},{5,4},{6,7},{7,6},{8,9},{9,8},{10,11... | collective-permute-start | bytes 491528 | tf_op jit(solution)/shard_map/ppermute | solution.py:66
  210.9 102.9 %copy-start.67 = (f32[128]{0:T(128)S(1)}, f32[128]{0:T(128)}, u32[]{:S(2)}) copy-start(f32[128]{0:T(128)} %copy-done.66) | copy-start | bytes 1540
  210.9 102.9 %copy-start.69 = (f32[128]{0:T(128)S(1)}, f32[128]{0:T(128)}, u32[]{:S(2)}) copy-start(f32[128]{0:T(128)} %copy-done.68) | copy-start | bytes 1540
  210.9 103.3 %copy-start.18 = (f32[128,256]{1,0:T(8,128)S(1)}, f32[128,256]{1,0:T(8,128)}, u32[]{:S(2)}) copy-start(f32[128,256]{1,0:T(8,128)} %copy-done.17) | copy-start | bytes 393220
  210.9 103.3 %copy-start.62 = (f32[128]{0:T(128)S(1)}, f32[128]{0:T(128)}, u32[]{:S(2)}) copy-start(f32[128]{0:T(128)} %copy-done.61) | copy-start | bytes 1540
  211.0 103.5 %copy-start.47 = (bf16[640,128]{1,0:T(8,128)(2,1)S(1)}, bf16[640,128]{1,0:T(8,128)(2,1)}, u32[]{:S(2)}) copy-start(bf16[640,128]{1,0:T(8,128)(2,1)} %param.20) | copy-start | bytes 491524
  211.0 103.5 %copy-start.52 = (bf16[640,128]{1,0:T(8,128)(2,1)S(1)}, bf16[640,128]{1,0:T(8,128)(2,1)}, u32[]{:S(2)}) copy-start(bf16[640,128]{1,0:T(8,128)(2,1)} %copy-done.51) | copy-start | bytes 491524
  211.0 103.8 %copy-start.48 = (bf16[640,128]{1,0:T(8,128)(2,1)S(1)}, bf16[640,128]{1,0:T(8,128)(2,1)}, u32[]{:S(2)}) copy-start(bf16[640,128]{1,0:T(8,128)(2,1)} %param.21) | copy-start | bytes 491524
  211.0 103.8 %copy-start.50 = (bf16[640,128]{1,0:T(8,128)(2,1)S(1)}, bf16[640,128]{1,0:T(8,128)(2,1)}, u32[]{:S(2)}) copy-start(bf16[640,128]{1,0:T(8,128)(2,1)} %copy-done.49) | copy-start | bytes 491524
  211.0 103.8 %copy-start.65 = (f32[128]{0:T(128)S(1)}, f32[128]{0:T(128)}, u32[]{:S(2)}) copy-start(f32[128]{0:T(128)} %copy-done.64) | copy-start | bytes 1540
  315.4 1.2 collective-permute-start.10
  315.5 1.5 collective-permute-start.9
  319.9 119.3 %all-to-all-start.1 = ((bf16[64,2,1300]{2,1,0:T(2,128)(2,1)}), bf16[64,2,1300]{2,1,0:T(2,128)(2,1)S(1)}, u32[]{:S(2)}, u32[]{:S(2)}) async-start(bf16[64,2,1300]{2,1,0:T(2,128)(2,1)} %reshape.477), calls=%async_computation.1 | async-start | bytes 720896 | tf_op jit(solution)/shard_map/all_to_all | solution.py:102
  444.6 19.3 %all-to-all-start.2 = ((bf16[64,2,1300]{2,1,0:T(2,128)(2,1)}), bf16[64,2,1300]{2,1,0:T(2,128)(2,1)S(1)}, u32[]{:S(2)}, u32[]{:S(2)}) async-start(bf16[64,2,1300]{2,1,0:T(2,128)(2,1)} %reshape.479), calls=%async_computation.2 | async-start | bytes 720896 | tf_op jit(solution)/shard_map/all_to_all | solution.py:105
  (67 other events, 717.4 us)
Sparse Core Ops, SparseCore 0:
  20.7 81.1 all-gather.1
  208.0 221.1 all-reduce.3
where the time goes:
time: 485 us; the launch traced here: 477 us
  waiting for transfers between devices  285 us (59%)
  matrix products  82.5 us (17%)
  other arithmetic  42.9 us (9%)
  starting transfers between devices  30.8 us (6%)
  local copies, waits for them, and re-layouts  19.3 us (4%)
  between operations  15.9 us (3%)
    psum x1, waiting for transfers between devices, per_device(): lax.psum(big, CTX)  101 us
    all_to_all x1, waiting for transfers between devices, scatter_sum(): lax.all_to_all(parts.reshape(64, 128, -1), CTX, split_axis=0, concat_axis...  97.9 us
    all_gather x1, waiting for transfers between devices, gather_ctx(): return lax.all_gather(block, CTX, axis=0, tiled=True)  75.5 us
    dot_general x14, matrix products, dot_nt(): lax.dot_general(left, right, (((1,), (1,)), ((), ())), preferred_element_...  35.6 us
    dot_general x14, matrix products, dot_f32(): return jnp.dot(left, right, preferred_element_type=f32)  31.8 us
    dot_general x8, matrix products, dot_tn(): lax.dot_general(left, right, (((0,), (0,)), ((), ())), preferred_element_...  15.1 us
    all_to_all x1, waiting for transfers between devices, small_sum(): out = lax.all_to_all(wide, CTX, split_axis=0, concat_axis=0, tiled=True)  10.7 us
    convert_element_type x5, other arithmetic, per_device(): g.astype(f32)  9.98 us
  transfers between devices with their start and end apart: 23, of which 6 were waited for; matrix products, arithmetic and copies ran while one was open for 18% of the time, Pallas kernels for 0%

commit v1 on v0

--- a/solution.py
+++ b/solution.py
@@ -243,7 +243,9 @@
     big = tuple(
         (g.astype(bf16) for g in (grad_w_query, grad_w_out, grad_w_gate, grad_w_up, grad_w_down))
     )
-    sum_query, sum_out, sum_gate, sum_up, sum_down = (g.astype(f32) for g in lax.psum(big, CTX))
+    sum_query, sum_out, sum_gate, sum_up, sum_down = (
+        g.astype(f32) for g in lax.psum(lax.psum(big, axis_name="z"), axis_name=("x", "y"))
+    )
     kv_mine = scatter_sum(kv_terms)
     grad_key_raw, grad_gain_key = rms_backward(
         key_raw, key_factor, gain_key, rotate_back(kv_mine[:, :HDIM], cos_tab, sin_tab)

time: 485 us -> 533 us (1.099)
  waiting for transfers between devices: 285 us -> 321 us
  blocking collectives: 0 us -> 24.9 us
  starting transfers between devices: 30.8 us -> 19.1 us
    psum x1 -> x2, waiting for transfers between devices: 101 us -> 234 us  [the longest x1 176 us: per_device(): lax.psum(big, axis_name='z')]
    all_to_all x1, waiting for transfers between devices: 97.9 us -> 0.01 us  [scatter_sum(): lax.all_to_all(parts.reshape(64, 128, -1), CTX, split_axis=0, concat_axis...]
    all_to_all x0 -> x1, blocking collectives: none -> 24.9 us  [small_sum(): lax.all_to_all(values.reshape(64, rows, -1), CTX, split_axis=0, concat_ax...]
    all_to_all x1 -> x0, starting transfers between devices: 8.71 us -> none  [small_sum(): lax.all_to_all(values.reshape(64, rows, -1), CTX, split_axis=0, concat_ax...]
  transfers between devices with their start and end apart: 23 -> 23, of which waited for: 6 -> 6; matrix products, arithmetic and copies ran while one was open for 18% -> 16% of each run, Pallas kernels for 0% -> 0%
where the time goes in v1:
time: 533 us; the launch traced here: 524 us
  waiting for transfers between devices  321 us (60%)
  matrix products  82.5 us (15%)
  other arithmetic  43 us (8%)
  blocking collectives  24.9 us (5%)
  starting transfers between devices  19.1 us (4%)
  local copies, waits for them, and re-layouts  18.6 us (3%)
  between operations  15.6 us (3%)
    psum x1, waiting for transfers between devices, per_device(): lax.psum(big, axis_name='z')  176 us
    all_gather x1, waiting for transfers between devices, gather_ctx(): return lax.all_gather(block, CTX, axis=0, tiled=True)  75.5 us
    psum x1, waiting for transfers between devices, per_device(): lax.psum(lax.psum(big, axis_name='z'), axis_name=('x', 'y'))  58.5 us
    dot_general x14, matrix products, dot_nt(): lax.dot_general(left, right, (((1,), (1,)), ((), ())), preferred_element_...  35.6 us
    dot_general x14, matrix products, dot_f32(): return jnp.dot(left, right, preferred_element_type=f32)  31.8 us
    all_to_all x1, blocking collectives, small_sum(): lax.all_to_all(values.reshape(64, rows, -1), CTX, split_axis=0, concat_ax...  24.9 us
    dot_general x8, matrix products, dot_tn(): lax.dot_general(left, right, (((0,), (0,)), ((), ())), preferred_element_...  15.1 us
  transfers between devices with their start and end apart: 23, of which 6 were waited for; matrix products, arithmetic and copies ran while one was open for 16% of the time, Pallas kernels for 0%

profile of v1, /device:TPU:0, one launch (start us, length us, event | category | flops | bytes accessed | tf_op | source)
XLA Modules:
  0.0 524.4 jit_solution(12488105035314445632)
XLA Ops:
  7.2 4.3 concatenate.211
  26.4 75.5 %all-gather.2.cloned.1.call-done = bf16[8192,512]{1,0:T(8,128)(2,1)} async-done(((bf16[128,512]{1,0:T(8,128)(2,1)}), bf16[8192,512]{1,0:T(8,128)(2,1)}) %all-gather.2.cloned.1.call-update) | async-done | bytes 8388624 | tf_op jit(solution)/shard_map/all_gather | solution.py:92
  101.9 10.8 %fusion.133 = (f32[512]{0:T(512)S(1)}, f32[512,8192]{1,0:T(8,128)}) fusion(bf16[8192,512]{1,0:T(8,128)(2,1)} %all-gather.2.cloned.1.call-done, bf16[512,128]{1,0:T(8,128)(2,1)} %get-tuple-element.104, bf16[512,128]{1,0:T(8,128)(2,1)S(1)} %get-tuple-element.103, s32[512]{0:T(512)S(1)} %broadcast_bitcast_fusion, s32[8192]{0:T(1024)S(1)} %add.257), kind=kOutput, calls=%fused_computation.278 | convolution fusion | flops 2164784640 | bytes 21270528 | tf_op jit(solution)/shard_map/dot_general | solution.py:58
  112.8 8.1 %fusion = f32[512]{0:T(512)S(1)} fusion(f32[512,8192]{1,0:T(8,128)} %get-tuple-element.164, f32[512]{0:T(512)S(1)} %get-tuple-element.163), kind=kLoop, calls=%fused_computation.6 | loop fusion | flops 8388096 | bytes 16781312 | tf_op jit(solution)/shard_map/reduce_sum | solution.py:74
  120.9 10.0 %fusion.14 = bf16[512,256]{0,1:T(8,128)(2,1)S(1)} fusion(bf16[8192,512]{1,0:T(8,128)(2,1)} %all-gather.2.cloned.1.call-done, f32[512,8192]{1,0:T(8,128)} %get-tuple-element.164, f32[512]{0:T(512)S(1)} %fusion, f32[512]{0:T(512)S(1)} %get-tuple-element.163), kind=kOutput, calls=%fused_computation.27 | convolution fusion | flops 2160197632 | bytes 21237760 | tf_op jit(solution)/shard_map/dot_general | solution.py:54
  134.4 1.7 fusion.136
  137.0 1.8 fusion.138
  139.3 1.9 multiply_reduce_fusion.9
  143.6 2.0 fusion.139
  145.7 2.2 multiply_convert_fusion.2
  147.9 2.1 convolution_add_fusion.5
  156.1 5.2 convolution_convert_fusion
  161.3 10.0 %multiply_convert_fusion = bf16[512,8192]{1,0:T(8,128)(2,1)S(1)} fusion(f32[512,8192]{1,0:T(8,128)} %get-tuple-element.164, f32[512]{0:T(512)S(1)} %multiply_reduce_fusion.2, f32[512]{0:T(512)S(1)} %log_add_fusion, bf16[8192,512]{1,0:T(8,128)(2,1)} %all-gather.2.cloned.1.call-done, bf16[128,256]{0,1:T(8,128)(2,1)S(1)} %get-tuple-element.136, ...), kind=kOutput, calls=%fused_computation.1 | convolution fusion | flops 2165309440 | bytes 29626368 | tf_op jit(solution)/shard_map/dot_general | solution.py:58
  171.3 2.4 fusion.2
  173.7 1.8 copy-done.1
  176.6 4.4 copy_bitcast_fusion
  181.0 9.0 %all-to-all-start = ((bf16[64,128,512]{1,2,0:T(8,128)(2,1)}), bf16[64,128,512]{1,2,0:T(8,128)(2,1)}, u32[]{:S(2)}, u32[]{:S(2)}) async-start(bf16[64,128,512]{1,2,0:T(8,128)(2,1)} %copy_bitcast_fusion), calls=%async_computation | async-start | bytes 16777216 | tf_op jit(solution)/shard_map/all_to_all | solution.py:96
  190.2 6.9 %fusion.11 = f32[512,256]{1,0:T(8,128)S(1)} fusion(bf16[512,8192]{1,0:T(8,128)(2,1)} %copy-done.1, bf16[8192,512]{1,0:T(8,128)(2,1)} %all-gather.2.cloned.1.call-done), kind=kOutput, calls=%fused_computation.26 | convolution fusion | flops 2147614720 | bytes 13107200 | tf_op jit(solution)/shard_map/dot_general | solution.py:54
  203.0 1.6 convolution_convert_fusion.3
  206.2 1.7 convolution_convert_fusion.1
  211.0 175.8 %all-reduce.8.cloned.1.call-done = (bf16[640,512]{1,0:T(8,128)(2,1)}, bf16[512,640]{1,0:T(8,128)(2,1)}, bf16[640,1024]{1,0:T(8,128)(2,1)}, bf16[640,1024]{1,0:T(8,128)(2,1)}, bf16[1024,640]{1,0:T(8,128)(2,1)}) async-done(((bf16[640,512]{1,0:T(8,128)(2,1)}, bf16[512,640]{1,0:T(8,128)(2,1)}, bf16[640,1024]{1,0:T(8,128)(2,1)}, bf16[640,1024]{1,0:T(8,128)(2,1)}, bf16[1024,640]{1,0:T(8,128)(2,1)}), ...) | async-done | bytes 5242896 | tf_op jit(solution)/shard_map/psum | solution.py:247
  386.9 4.8 convert_reduce_fusion
  397.2 24.9 %all_to_all.15 = bf16[64,2,1300]{2,1,0:T(2,128)(2,1)S(1)} all-to-all(bf16[64,2,1300]{2,1,0:T(2,128)(2,1)S(1)} %reshape.477), channel_id=1, replica_groups=mesh['z'=4,'x'=4,'y'=4,'wsh'=2] {'z','x','y'}, dimensions={0} | all-to-all | bytes 665600 | tf_op jit(solution)/shard_map/all_to_all | solution.py:102
  423.6 2.8 reduce.22
  427.5 4.7 all-to-all-start.2
  433.1 10.2 %all-to-all-done.2 = bf16[64,2,1300]{2,1,0:T(2,128)(2,1)S(1)} async-done(((bf16[64,2,1300]{2,1,0:T(2,128)(2,1)}), bf16[64,2,1300]{2,1,0:T(2,128)(2,1)S(1)}, u32[]{:S(2)}, u32[]{:S(2)}) %all-to-all-start.2) | async-done | bytes 332832 | tf_op jit(solution)/shard_map/all_to_all | solution.py:105
  449.2 58.5 %all-reduce.6.cloned.1.call-done = (bf16[640,512]{1,0:T(8,128)(2,1)}, bf16[512,640]{1,0:T(8,128)(2,1)}, bf16[640,1024]{1,0:T(8,128)(2,1)}, bf16[640,1024]{1,0:T(8,128)(2,1)}, bf16[1024,640]{1,0:T(8,128)(2,1)}) async-done(((bf16[640,512]{1,0:T(8,128)(2,1)}, bf16[512,640]{1,0:T(8,128)(2,1)}, bf16[640,1024]{1,0:T(8,128)(2,1)}, bf16[640,1024]{1,0:T(8,128)(2,1)}, bf16[1024,640]{1,0:T(8,128)(2,1)}), ...) | async-done | bytes 5242896 | tf_op jit(solution)/shard_map/psum | solution.py:247
  507.7 2.5 convert_element_type.209
  510.2 2.2 convert_element_type.215
  512.4 1.8 convert_element_type.217
  514.2 1.8 convert_element_type.219
  516.0 1.7 convert_element_type.221
  (325 shorter events, 53.6 us)
Async XLA Ops:
  7.2 14.7 %copy-start.63 = (s32[64,2]{0,1:T(2,128)S(1)}, s32[64,2]{0,1:T(2,128)}, u32[]{:S(2)}) copy-start(s32[64,2]{0,1:T(2,128)} %param.18) | copy-start | bytes 1540
  7.2 14.2 %copy-start.2 = (bf16[640,1024]{1,0:T(8,128)(2,1)S(1)}, bf16[640,1024]{1,0:T(8,128)(2,1)}, u32[]{:S(2)}) copy-start(bf16[640,1024]{1,0:T(8,128)(2,1)} %param.24) | copy-start | bytes 3932164
  7.2 94.7 %all-gather.2.cloned.1.call-start = ((), (), s32[]{:S(2)}) async-start(), calls=%async_computation.3 | async-start | bytes 8519680 | tf_op jit(solution)/shard_map/all_gather | solution.py:92
  11.5 3.9 collective-permute-start
  12.7 4.0 collective-permute-start.2
  19.9 92.9 %copy-start.27 = (f32[128,128]{1,0:T(8,128)}, f32[128,128]{1,0:T(8,128)S(1)}, u32[]{:S(2)}) copy-start(f32[128,128]{1,0:T(8,128)S(1)} %get-tuple-element.157) | copy-start | bytes 196612
  19.9 92.9 %copy-start.29 = (f32[128,128]{1,0:T(8,128)}, f32[128,128]{1,0:T(8,128)S(1)}, u32[]{:S(2)}) copy-start(f32[128,128]{1,0:T(8,128)S(1)} %get-tuple-element.158) | copy-start | bytes 196612
  20.6 3.4 collective-permute-start.1
  20.7 111.9 %collective-permute-start.3 = (bf16[512,640]{1,0:T(8,128)(2,1)}, bf16[512,640]{1,0:T(8,128)(2,1)}, u32[]{:S(2)}, u32[]{:S(2)}) collective-permute-start(bf16[512,640]{1,0:T(8,128)(2,1)} %param.22), channel_id=1, source_target_pairs={{0,1},{1,0},{2,3},{3,2},{4,5},{5,4},{6,7},{7,6},{8,9},{9,8},{10,11... | collective-permute-start | bytes 1966088 | tf_op jit(solution)/shard_map/ppermute | solution.py:66
  21.2 115.8 %collective-permute-start.4 = (bf16[640,1024]{1,0:T(8,128)(2,1)}, bf16[640,1024]{1,0:T(8,128)(2,1)}, u32[]{:S(2)}, u32[]{:S(2)}) collective-permute-start(bf16[640,1024]{1,0:T(8,128)(2,1)} %param.23), channel_id=1, source_target_pairs={{0,1},{1,0},{2,3},{3,2},{4,5},{5,4},{6,7},{7,6},{8,9},{9,8},{10,11... | collective-permute-start | bytes 3932168 | tf_op jit(solution)/shard_map/ppermute | solution.py:66
  21.4 117.5 %collective-permute-start.5 = (bf16[640,1024]{1,0:T(8,128)(2,1)S(1)}, bf16[640,1024]{1,0:T(8,128)(2,1)S(1)}, u32[]{:S(2)}, u32[]{:S(2)}) collective-permute-start(bf16[640,1024]{1,0:T(8,128)(2,1)S(1)} %copy-done.2), channel_id=1, source_target_pairs={{0,1},{1,0},{2,3},{3,2},{4,5},{5,4},{6,7},{7,6},{8,9},{9,8},{10,11... | collective-permute-start | bytes 3932168 | tf_op jit(solution)/shard_map/ppermute | solution.py:66
  21.8 117.5 %collective-permute-start.6 = (bf16[1024,640]{1,0:T(8,128)(2,1)}, bf16[1024,640]{1,0:T(8,128)(2,1)}, u32[]{:S(2)}, u32[]{:S(2)}) collective-permute-start(bf16[1024,640]{1,0:T(8,128)(2,1)} %param.25), channel_id=1, source_target_pairs={{0,1},{1,0},{2,3},{3,2},{4,5},{5,4},{6,7},{7,6},{8,9},{9,8},{10,11... | collective-permute-start | bytes 3932168 | tf_op jit(solution)/shard_map/ppermute | solution.py:66
  22.5 90.3 %copy-start.59 = (f32[256]{0:T(256)}, f32[256]{0:T(256)S(1)}, u32[]{:S(2)}) copy-start(f32[256]{0:T(256)S(1)} %convert_add_fusion.6) | copy-start | bytes 3076
  26.4 86.4 %copy-start.55 = (bf16[512,128]{1,0:T(8,128)(2,1)}, bf16[512,128]{1,0:T(8,128)(2,1)S(1)}, u32[]{:S(2)}) copy-start(bf16[512,128]{1,0:T(8,128)(2,1)S(1)} %get-tuple-element.103) | copy-start | bytes 393220
  137.0 19.1 %slice-start = ((s8[16777216]{0:T(1024)(128)(4,1)}), s8[4194304]{0:T(1024)(128)(4,1)S(1)}, s32[]{:S(2)}) async-start(s8[16777216]{0:T(1024)(128)(4,1)} %bitcast.111), calls=%async_computation.6 | async-start | bytes 8388608
  141.9 14.2 %slice-start.1 = ((s8[16777216]{0:T(1024)(128)(4,1)}), s8[4194304]{0:T(1024)(128)(4,1)S(1)}, s32[]{:S(2)}) async-start(s8[16777216]{0:T(1024)(128)(4,1)} %bitcast.111), calls=%async_computation.7 | async-start | bytes 8388608
  181.0 205.9 %all-to-all-start = ((bf16[64,128,512]{1,2,0:T(8,128)(2,1)}), bf16[64,128,512]{1,2,0:T(8,128)(2,1)}, u32[]{:S(2)}, u32[]{:S(2)}) async-start(bf16[64,128,512]{1,2,0:T(8,128)(2,1)} %copy_bitcast_fusion), calls=%async_computation | async-start | bytes 16777216 | tf_op jit(solution)/shard_map/all_to_all | solution.py:96
  190.0 196.7 %all-reduce.8.cloned.1.call-start = ((), (), s32[]{:S(2)}) async-start(), calls=%async_computation.5 | async-start | bytes 10485760 | tf_op jit(solution)/shard_map/psum | solution.py:247
  190.1 9.1 %collective-permute-start.7 = (bf16[128,640]{1,0:T(8,128)(2,1)S(1)}, bf16[128,640]{1,0:T(8,128)(2,1)S(1)}, u32[]{:S(2)}, u32[]{:S(2)}) collective-permute-start(bf16[128,640]{1,0:T(8,128)(2,1)S(1)} %copy-done.10), channel_id=1, source_target_pairs={{0,1},{1,0},{2,3},{3,2},{4,5},{5,4},{6,7},{7,6},{8,9},{9,8},{10,11... | collective-permute-start | bytes 491528 | tf_op jit(solution)/shard_map/ppermute | solution.py:66
  197.9 1.7 collective-permute-start.8
  198.5 2.9 collective-permute-start.12
  198.6 4.4 collective-permute-start.14
  199.0 2.0 collective-permute-start.11
  199.2 3.8 collective-permute-start.13
  199.6 4.9 collective-permute-start.15
  201.1 5.1 collective-permute-start.16
  201.4 4.8 collective-permute-start.17
  207.9 299.8 %all-reduce.6.cloned.1.call-start = ((), (), s32[]{:S(2)}) async-start(), calls=%async_computation.4 | async-start | bytes 10485760 | tf_op jit(solution)/shard_map/psum | solution.py:247
  393.4 1.2 collective-permute-start.10
  393.5 1.5 collective-permute-start.9
  395.3 36.9 %copy-start.7 = (f32[128,640]{1,0:T(8,128)S(1)}, f32[128,640]{1,0:T(8,128)}, u32[]{:S(2)}) copy-start(f32[128,640]{1,0:T(8,128)} %copy-done.6) | copy-start | bytes 983044
  427.5 15.8 %all-to-all-start.2 = ((bf16[64,2,1300]{2,1,0:T(2,128)(2,1)}), bf16[64,2,1300]{2,1,0:T(2,128)(2,1)S(1)}, u32[]{:S(2)}, u32[]{:S(2)}) async-start(bf16[64,2,1300]{2,1,0:T(2,128)(2,1)} %reshape.479), calls=%async_computation.2 | async-start | bytes 720896 | tf_op jit(solution)/shard_map/all_to_all | solution.py:105
  (67 other events, 328.4 us)
Sparse Core Ops, SparseCore 0:
  20.7 81.1 all-gather.1
  208.0 178.6 all-reduce.7
  390.6 117.0 all-reduce.5
